TPU v7x, 512 devices: a whole 4x8x8 slice. The times are simulated.
512 devices in a mesh: vocab: 64 (over y, x, core), width: 8 (over z).
Axes of the slice: x: 4, y: 8, z: 8, core: 2. Of those that a mesh axis runs over, the one named last changes fastest.
Arguments:
- hidden: bfloat16 [8192, 2048], P('vocab', 'width'), may hold values from -400 to 400
- norm_gain: bfloat16 [2048], P('width'), may hold values from 0.5 to 1.5
- head_weight: bfloat16 [102400, 2048], P('vocab', 'width'), may hold values from -1 to 1
- targets: int32 [8192], P(('vocab', 'width')), may hold values from 0 to 102399
- pad_mask: int32 [8192], P(('vocab', 'width')), may hold values 0 or 1
- lengths: int32 [64], replicated, may hold values from 1 to 2048, 8192 in all
Outputs:
- entropy: float32 [8192], P(('vocab', 'width'))
- token_logprob: float32 [8192], P(('vocab', 'width'))
- seq_score: float32 [64], replicated
Inputs may be any that keep to these rules, and one draw needn't show every extreme that they name: The lengths sum to 8192.
All inputs are finite; a program needn't handle non-finite values. No bound on the sum of `pad_mask` on one device may be relied on, other than what follows from the above.
Results may differ from a plain program's by a relative error of at most 0.0031.
Values may be sent and summed in bfloat16 or wider, within the bound.
A program may use at most 64 MiB of HBM per device.

v0:
```python
import math
import jax
import jax.numpy as jnp
from jax import lax
from jax.sharding import PartitionSpec as P

epsilon = 1e-06


def merged_2(value, axis, join):
    pieces = jax.tree.map(lambda part: lax.all_gather(part, axis), value)
    head = jax.tree.map(lambda part: part[0], pieces)
    tail = jax.tree.map(lambda part: part[1:], pieces)
    total, _ = lax.scan(lambda total, piece: (join(total, piece), None), head, tail)
    return total


def summarize(logits, block_ids, first_col):
    peak = jnp.max(logits, axis=1)
    shifted = logits - peak[:, None]
    weights = jnp.exp(shifted)
    exp_total = jnp.sum(weights, axis=1)
    spread = jnp.sum(weights * shifted, axis=1)
    columns = first_col + lax.iota(jnp.int32, logits.shape[1])
    target_logit = jnp.sum(jnp.where(columns[None, :] == block_ids[:, None], logits, 0.0), axis=1)
    return (peak, exp_total, spread, target_logit)


def combine(earlier, later):
    peak = jnp.maximum(earlier[0], later[0])
    left_lift = jnp.exp(earlier[0] - peak)
    right_lift = jnp.exp(later[0] - peak)
    exp_total = earlier[1] * left_lift + later[1] * right_lift
    spread = left_lift * (earlier[2] + (earlier[0] - peak) * earlier[1]) + right_lift * (
        later[2] + (later[0] - peak) * later[1]
    )
    return (peak, exp_total, spread, earlier[3] + later[3])


def per_device(hidden, norm_gain, head_weight, targets, pad_mask, lengths):
    width_count = lax.axis_size("width")
    own_count = targets.shape[0]
    values = hidden.astype(jnp.float32)
    energy = lax.psum(jnp.sum(values * values, axis=1), "width")
    inv_rms = lax.rsqrt(energy / (hidden.shape[1] * width_count) + epsilon)
    normed = (values * inv_rms[:, None] * norm_gain.astype(jnp.float32)[None, :]).astype(
        jnp.bfloat16
    )
    full_rows = lax.all_to_all(normed, "width", split_axis=0, concat_axis=1, tiled=True)
    gathered, gathered_ids = (
        lax.all_gather(full_rows, "vocab", axis=0, tiled=True),
        lax.all_gather(targets, "vocab", axis=0, tiled=True),
    )
    col_count = head_weight.shape[0]
    first_col = lax.axis_index("vocab") * col_count
    total_rows = gathered.shape[0]
    block_rows = math.gcd(total_rows, 512)
    contract = (((1,), (1,)), ((), ()))
    head_full = lax.all_gather(head_weight, "width", axis=1, tiled=True)

    def per_block(inputs):
        logits = lax.dot_general(inputs[0], head_full, contract, preferred_element_type=jnp.float32)
        return summarize(logits, inputs[1], first_col)

    blocked = lax.map(
        per_block,
        (gathered.reshape(-1, block_rows, gathered.shape[1]), gathered_ids.reshape(-1, block_rows)),
    )
    statistics = (
        blocked[0].reshape(-1),
        blocked[1].reshape(-1),
        blocked[2].reshape(-1),
        blocked[3].reshape(-1),
    )
    merged = merged_2(statistics, "vocab", combine)
    own_start = lax.axis_index("vocab") * own_count
    peak = lax.dynamic_slice_in_dim(merged[0], own_start, own_count, 0)
    exp_total = lax.dynamic_slice_in_dim(merged[1], own_start, own_count, 0)
    spread = lax.dynamic_slice_in_dim(merged[2], own_start, own_count, 0)
    target_logit = lax.dynamic_slice_in_dim(merged[3], own_start, own_count, 0)
    kept_mask = pad_mask.astype(jnp.float32)
    log_total = jnp.log(exp_total)
    entropy = kept_mask * (log_total - spread / exp_total)
    token_logprob = kept_mask * (target_logit - peak - log_total)
    device_index = lax.axis_index("vocab") * width_count + lax.axis_index("width")
    token_index = device_index * own_count + lax.iota(jnp.int32, own_count)
    seq_ends = jnp.cumsum(lengths)
    seq_starts = seq_ends - lengths
    member = (
        (token_index[:, None] >= seq_starts[None, :]) & (token_index[:, None] < seq_ends[None, :])
    ).astype(jnp.float32)
    partial_value = jnp.sum(member * token_logprob[:, None], axis=0)
    seq_score = lax.psum(partial_value, ("vocab", "width")) / lengths.astype(jnp.float32)
    return (entropy, token_logprob, seq_score)


def solution(mesh):
    placed = (
        P("vocab", "width"),
        P("width"),
        P("vocab", "width"),
        P(("vocab", "width")),
        P(("vocab", "width")),
        P(),
    )
    return jax.shard_map(
        per_device,
        mesh=mesh,
        in_specs=placed,
        out_specs=(P(("vocab", "width")), P(("vocab", "width")), P()),
        check_vma=False,
    )
```

profile of v0, /device:TPU:1, one launch (start us, length us, event | category | flops | bytes accessed | tf_op | source)
XLA Modules:
  0.0 491.1 jit_solution(4575408305845917003)
XLA Ops:
  7.2 0.9 fusion.5
  8.2 20.3 %psum.14 = f32[128]{0:T(128)S(1)} all-reduce(f32[128]{0:T(128)S(1)} %fusion.5), channel_id=1, replica_groups=mesh['vocab'=64,'width'=8] {'width'}, use_global_device_ids=true, to_apply=%region_1.0 | all-reduce | flops 128 | bytes 1024 | tf_op jit(solution)/shard_map/psum | solution.py:44
  28.4 0.7 convert_element_type.18
  29.1 0.9 fusion.7
  30.0 9.6 %all_to_all.19 = bf16[8,16,256]{2,1,0:T(8,128)(2,1)S(1)} all-to-all(bf16[8,16,256]{2,1,0:T(8,128)(2,1)S(1)} %bitcast.73), channel_id=1, replica_groups=mesh['vocab'=64,'width'=8] {'width'}, dimensions={0} | all-to-all | bytes 131072 | tf_op jit(solution)/shard_map/all_to_all | solution.py:49
  40.3 0.7 all-gather.9.cloned.1.call-update
  41.1 1.3 dynamic-slice
  43.0 0.9 dynamic-update-slice
  43.9 22.5 %all-reduce = s32[1024]{0:T(1024)S(1)} all-reduce(s32[1024]{0:T(1024)S(1)} %dynamic-update-slice), channel_id=1, replica_groups=mesh['vocab'=64,'width'=8] {'vocab'}, use_global_device_ids=true, to_apply=%add | all-reduce | flops 1024 | bytes 8192
  66.4 0.7 copy.16
  67.4 0.7 sub.31
  68.0 58.4 %all-gather.7.cloned.1.call-done = bf16[1024,2048]{1,0:T(8,128)(2,1)} async-done(((bf16[16,2048]{1,0:T(8,128)(2,1)}), bf16[1024,2048]{1,0:T(8,128)(2,1)}) %all-gather.7.cloned.1.call-update) | async-done | bytes 4194320 | tf_op jit(solution)/shard_map/all_gather | solution.py:51
  126.4 83.2 %all-gather.9.cloned.1.call-done = bf16[1600,2048]{1,0:T(8,128)(2,1)} async-done(((bf16[1600,256]{1,0:T(8,128)(2,1)}), bf16[1600,2048]{1,0:T(8,128)(2,1)}) %all-gather.9.cloned.1.call-update) | async-done | bytes 6553616 | tf_op jit(solution)/shard_map/all_gather | solution.py:59
  209.6 16.2 %while.32 = (s32[]{:T(128)}, f32[2,512]{1,0:T(2,128)S(1)}, f32[2,512]{1,0:T(2,128)S(1)}, f32[2,512]{1,0:T(2,128)S(1)}, f32[2,512]{1,0:T(2,128)S(1)}, /*index=5*/...) while((s32[]{:T(128)}, f32[2,512]{1,0:T(2,128)S(1)}, ...), condition=%wide.region_7.8_spmd, body=%wide.region_2.7_spmd.sunk | while | flops 3361996288 | bytes 15250565 | solution.py:65
  209.6 6.4 %fusion.14 = (f32[512]{0:T(512)S(1)}, f32[512,1600]{0,1:T(8,128)S(1)}) fusion(bf16[1600,2048]{1,0:T(8,128)(2,1)} %get-tuple-element.320, bf16[2,512,2048]{2,1,0:T(8,128)(2,1)} %get-tuple-element.319, s32[]{:T(128)} %get-tuple-element.303), kind=kOutput, calls=%fused_computation.31.clone.1 | convolution fusion | flops 3356261888 | bytes 11930112 | tf_op jit(solution)/shard_map/while/body/eval_jaxpr/dot_general | solution.py:62
  216.1 1.4 fusion.15
  217.7 6.4 %fusion.14 = (f32[512]{0:T(512)S(1)}, f32[512,1600]{0,1:T(8,128)S(1)}) fusion(bf16[1600,2048]{1,0:T(8,128)(2,1)} %get-tuple-element.320, bf16[2,512,2048]{2,1,0:T(8,128)(2,1)} %get-tuple-element.319, s32[]{:T(128)} %get-tuple-element.303), kind=kOutput, calls=%fused_computation.31.clone.1 | convolution fusion | flops 3356261888 | bytes 11930112 | tf_op jit(solution)/shard_map/while/body/eval_jaxpr/dot_general | solution.py:62
  224.2 1.4 fusion.15
  225.8 42.7 %all-gather = f32[64,1,1024]{2,1,0:T(1,128)S(1)} all-gather(f32[1,1,1024]{2,1,0:T(1,128)S(1)} %reshape.60), channel_id=1, replica_groups=mesh['vocab'=64,'width'=8] {'vocab'}, dimensions={0}, use_global_device_ids=true | all-gather | bytes 266240 | tf_op jit(solution)/shard_map/all_gather | solution.py:11
  268.6 37.2 %all-gather.1 = f32[64,1,1024]{2,1,0:T(1,128)S(1)} all-gather(f32[1,1,1024]{2,1,0:T(1,128)S(1)} %reshape.62), channel_id=1, replica_groups=mesh['vocab'=64,'width'=8] {'vocab'}, dimensions={0}, use_global_device_ids=true | all-gather | bytes 266240 | tf_op jit(solution)/shard_map/all_gather | solution.py:11
  305.8 36.9 %all-gather.2 = f32[64,1,1024]{2,1,0:T(1,128)S(1)} all-gather(f32[1,1,1024]{2,1,0:T(1,128)S(1)} %reshape.64), channel_id=1, replica_groups=mesh['vocab'=64,'width'=8] {'vocab'}, dimensions={0}, use_global_device_ids=true | all-gather | bytes 266240 | tf_op jit(solution)/shard_map/all_gather | solution.py:11
  342.7 37.1 %all-gather.3 = f32[64,1,1024]{2,1,0:T(1,128)S(1)} all-gather(f32[1,1,1024]{2,1,0:T(1,128)S(1)} %reshape.66), channel_id=1, replica_groups=mesh['vocab'=64,'width'=8] {'vocab'}, dimensions={0}, use_global_device_ids=true | all-gather | bytes 266240 | tf_op jit(solution)/shard_map/all_gather | solution.py:11
  380.2 7.6 %while.33 = (s32[]{:T(128)}, f32[1024]{0:T(1024)S(1)}, f32[1024]{0:T(1024)S(1)}, f32[1024]{0:T(1024)S(1)}, f32[1024]{0:T(1024)S(1)}, /*index=5*/f32[63,1024]{1,0...) while((s32[]{:T(128)}, f32[1024]{0:T(1024)S(1)}, ...), condition=%wide.region_9.10_spmd, body=%wide.region_8.9_spmd.sunk | while | flops 16386 | bytes 110701 | solution.py:14
  388.4 95.3 %psum.15 = f32[64]{0:T(128)S(1)} all-reduce(f32[64]{0:T(128)S(1)} %select_reduce_fusion.1), channel_id=1, replica_groups=mesh['vocab'=64,'width'=8] {'vocab','width'}, use_global_device_ids=true, to_apply=%region_12.13 | all-reduce | flops 64 | bytes 512 | tf_op jit(solution)/shard_map/psum | solution.py:93
  (429 shorter events, 6.7 us)
Async XLA Ops:
  7.2 119.3 %all-gather.7.cloned.1.call-start = ((), (), s32[]{:S(2)}) async-start(), calls=%async_computation.1 | async-start | bytes 4259840 | tf_op jit(solution)/shard_map/all_gather | solution.py:51
  40.3 169.3 %all-gather.9.cloned.1.call-start = ((), (), s32[]{:S(2)}) async-start(), calls=%async_computation.2 | async-start | bytes 7372800 | tf_op jit(solution)/shard_map/all_gather | solution.py:59
  225.8 162.0 %copy-start.2 = (s32[16]{0:T(128)S(1)}, s32[16]{0:T(128)}, u32[]{:S(2)}) copy-start(s32[16]{0:T(128)} %param.14) | copy-start | bytes 196
  225.8 257.9 %copy-start.1 = (s32[64]{0:T(128)S(1)}, s32[64]{0:T(128)}, u32[]{:S(2)}) copy-start(s32[64]{0:T(128)} %param.15) | copy-start | bytes 772
  388.3 95.9 %copy-start = (f32[16]{0:T(128)}, f32[16]{0:T(128)S(1)}, u32[]{:S(2)}) copy-start(f32[16]{0:T(128)S(1)} %get-tuple-element.158) | copy-start | bytes 196
Sparse Core Ops, SparseCore 0:
  40.4 85.9 all-gather.6
  128.4 81.1 all-gather.8
where the time goes:
time: 491 us
  blocking collectives  302 us (62%)
  waiting for transfers between devices  142 us (29%)
  between operations  14.9 us (3%)
  matrix products  12.9 us (3%)
  other arithmetic  9.19 us (2%)
  local copies, waits for them, and re-layouts  6.36 us (1%)
    all_gather x4, blocking collectives, merged_2(): pieces = jax.tree.map(lambda part: lax.all_gather(part, axis), value)  154 us
    psum x1, blocking collectives, per_device(): lax.psum(partial_value, ('vocab', 'width')) / lengths.astype(jnp.float32)  95.3 us
    all_gather x1, waiting for transfers between devices, per_device(): head_full = lax.all_gather(head_weight, 'width', axis=1, tiled=True)  83.2 us
    all_gather x1, waiting for transfers between devices, per_device(): lax.all_gather(full_rows, 'vocab', axis=0, tiled=True)  58.4 us
    unnamed x1, blocking collectives  22.5 us
    psum x1, blocking collectives, per_device(): energy = lax.psum(jnp.sum(values * values, axis=1), 'width')  20.3 us
    dot_general x2, matrix products, per_block(): lax.dot_general(inputs[0], head_full, contract, preferred_element_type=jn...  12.9 us
  transfers between devices with their start and end apart: 2, of which 2 were waited for; matrix products, arithmetic and copies ran while one was open for 1% of the time, Pallas kernels for 0%

commit v1 on v0

--- a/solution.py
+++ b/solution.py
@@ -56,7 +56,14 @@
     total_rows = gathered.shape[0]
     block_rows = math.gcd(total_rows, 512)
     contract = (((1,), (1,)), ((), ()))
-    head_full = lax.all_gather(head_weight, "width", axis=1, tiled=True)
+    ring = [head_weight]
+    for hop in range(7):
+        ring.append(lax.ppermute(ring[-1], "width", [(dev, (dev + 1) % 8) for dev in range(8)]))
+    head_full = jnp.roll(
+        jnp.concatenate(ring[::-1], axis=1),
+        (lax.axis_index("width") + 1) * ring[0].shape[1],
+        axis=1,
+    )
 
     def per_block(inputs):
         logits = lax.dot_general(inputs[0], head_full, contract, preferred_element_type=jnp.float32)

time: 491 us -> 465 us (0.947)
  waiting for transfers between devices: 142 us -> 65.6 us
  starting transfers between devices: 0.08 us -> 19.6 us
  local copies, waits for them, and re-layouts: 6.36 us -> 21.4 us
  blocking collectives: 302 us -> 317 us
    all_gather x1 -> x0, waiting for transfers between devices: 83.2 us -> none  [per_device(): head_full = lax.all_gather(head_weight, 'width', axis=1, tiled=True)]
    ppermute x0 -> x7, waiting for transfers between devices: none -> 65.6 us  [per_device(): lax.ppermute(ring[-1], 'width', [(dev, (dev + 1) % 8) for dev in range(8)])]
    all_gather x1, waiting for transfers between devices: 58.4 us -> 0.01 us  [per_device(): lax.all_gather(full_rows, 'vocab', axis=0, tiled=True)]
    ppermute x0 -> x7, starting transfers between devices: none -> 19.5 us  [per_device(): lax.ppermute(ring[-1], 'width', [(dev, (dev + 1) % 8) for dev in range(8)])]
    unnamed x17 -> x42, local copies, waits for them, and re-layouts: 2.41 us -> 14 us
    unnamed x1, blocking collectives: 22.5 us -> 30 us
    all_to_all x1, blocking collectives: 9.6 us -> 14.7 us  [per_device(): lax.all_to_all(normed, 'width', split_axis=0, concat_axis=1, tiled=True)]
  transfers between devices with their start and end apart: 2 -> 8, of which waited for: 2 -> 4; matrix products, arithmetic and copies ran while one was open for 1% -> 4% of each run, Pallas kernels for 0% -> 0%
where the time goes in v1:
time: 465 us; the launch traced here: 464 us
  blocking collectives  317 us (68%)
  waiting for transfers between devices  65.6 us (14%)
  local copies, waits for them, and re-layouts  21.4 us (5%)
  starting transfers between devices  19.6 us (4%)
  between operations  15.1 us (3%)
  matrix products  12.9 us (3%)
  other arithmetic  9.19 us (2%)
    all_gather x4, blocking collectives, merged_2(): pieces = jax.tree.map(lambda part: lax.all_gather(part, axis), value)  152 us
    psum x1, blocking collectives, per_device(): lax.psum(partial_value, ('vocab', 'width')) / lengths.astype(jnp.float32)  96.1 us
    ppermute x7, waiting for transfers between devices, per_device(): lax.ppermute(ring[-1], 'width', [(dev, (dev + 1) % 8) for dev in range(8)])  65.6 us
    unnamed x1, blocking collectives  30 us
    psum x1, blocking collectives, per_device(): energy = lax.psum(jnp.sum(values * values, axis=1), 'width')  23.9 us
    ppermute x7, starting transfers between devices, per_device(): lax.ppermute(ring[-1], 'width', [(dev, (dev + 1) % 8) for dev in range(8)])  19.5 us
    all_to_all x1, blocking collectives, per_device(): lax.all_to_all(normed, 'width', split_axis=0, concat_axis=1, tiled=True)  14.7 us
    unnamed x42, local copies, waits for them, and re-layouts  14 us
  transfers between devices with their start and end apart: 8, of which 4 were waited for; matrix products, arithmetic and copies ran while one was open for 4% of the time, Pallas kernels for 0%

profile of v1, /device:TPU:1, one launch (start us, length us, event | category | flops | bytes accessed | tf_op | source)
XLA Modules:
  0.0 464.4 jit_solution(8162286199095943899)
XLA Ops:
  7.2 5.0 %collective-permute-start = (bf16[1600,256]{1,0:T(8,128)(2,1)}, bf16[1600,256]{1,0:T(8,128)(2,1)S(1)}, u32[]{:S(2)}, u32[]{:S(2)}) collective-permute-start(bf16[1600,256]{1,0:T(8,128)(2,1)} %param.12), channel_id=1, source_target_pairs={{0,1},{1,2},{2,3},{3,4},{4,5},{5,6},{6,7},{7,0},{8,9},{9,10},{10,1... | collective-permute-start | bytes 2457608 | tf_op jit(solution)/shard_map/ppermute | solution.py:61
  12.2 24.8 %collective-permute-done = bf16[1600,256]{1,0:T(8,128)(2,1)S(1)} collective-permute-done((bf16[1600,256]{1,0:T(8,128)(2,1)}, bf16[1600,256]{1,0:T(8,128)(2,1)S(1)}, u32[]{:S(2)}, u32[]{:S(2)}) %collective-permute-start) | collective-permute-done | bytes 819232 | tf_op jit(solution)/shard_map/ppermute | solution.py:61
  37.0 1.9 collective-permute-start.1
  40.5 23.9 %psum.14 = f32[128]{0:T(128)S(1)} all-reduce(f32[128]{0:T(128)S(1)} %fusion.5), channel_id=1, replica_groups=mesh['vocab'=64,'width'=8] {'width'}, use_global_device_ids=true, to_apply=%region_1.0 | all-reduce | flops 128 | bytes 1024 | tf_op jit(solution)/shard_map/psum | solution.py:44
  64.4 3.4 collective-permute-start.2
  68.7 14.7 %all_to_all.19 = bf16[8,16,256]{2,1,0:T(8,128)(2,1)S(1)} all-to-all(bf16[8,16,256]{2,1,0:T(8,128)(2,1)S(1)} %bitcast.73), channel_id=1, replica_groups=mesh['vocab'=64,'width'=8] {'width'}, dimensions={0} | all-to-all | bytes 131072 | tf_op jit(solution)/shard_map/all_to_all | solution.py:49
  84.1 2.5 collective-permute-start.3
  86.6 13.6 %collective-permute-done.3 = bf16[1600,256]{1,0:T(8,128)(2,1)S(1)} collective-permute-done((bf16[1600,256]{1,0:T(8,128)(2,1)S(1)}, bf16[1600,256]{1,0:T(8,128)(2,1)S(1)}, u32[]{:S(2)}, u32[]{:S(2)}) %collective-permute-start.3) | collective-permute-done | bytes 819232 | tf_op jit(solution)/shard_map/ppermute | solution.py:61
  101.1 2.2 collective-permute-start.4
  103.3 13.6 %collective-permute-done.4 = bf16[1600,256]{1,0:T(8,128)(2,1)S(1)} collective-permute-done((bf16[1600,256]{1,0:T(8,128)(2,1)S(1)}, bf16[1600,256]{1,0:T(8,128)(2,1)S(1)}, u32[]{:S(2)}, u32[]{:S(2)}) %collective-permute-start.4) | collective-permute-done | bytes 819232 | tf_op jit(solution)/shard_map/ppermute | solution.py:61
  117.9 2.2 collective-permute-start.5
  120.1 13.5 %collective-permute-done.5 = bf16[1600,256]{1,0:T(8,128)(2,1)} collective-permute-done((bf16[1600,256]{1,0:T(8,128)(2,1)S(1)}, bf16[1600,256]{1,0:T(8,128)(2,1)}, u32[]{:S(2)}, u32[]{:S(2)}) %collective-permute-start.5) | collective-permute-done | bytes 819232 | tf_op jit(solution)/shard_map/ppermute | solution.py:61
  133.6 2.4 collective-permute-start.6
  138.8 30.0 %all-reduce = s32[1024]{0:T(1024)S(1)} all-reduce(s32[1024]{0:T(1024)S(1)} %dynamic-update-slice), channel_id=1, replica_groups=mesh['vocab'=64,'width'=8] {'vocab'}, use_global_device_ids=true, to_apply=%add | all-reduce | flops 1024 | bytes 8192
  180.5 3.4 constant_dynamic-slice_fusion.5
  183.9 16.2 %while.32 = (s32[]{:T(128)}, f32[2,512]{1,0:T(2,128)S(1)}, f32[2,512]{1,0:T(2,128)S(1)}, f32[2,512]{1,0:T(2,128)S(1)}, f32[2,512]{1,0:T(2,128)S(1)}, /*index=5*/...) while((s32[]{:T(128)}, f32[2,512]{1,0:T(2,128)S(1)}, ...), condition=%wide.region_7.8_spmd, body=%wide.region_2.7_spmd.sunk | while | flops 3361996288 | bytes 15250565 | solution.py:72
  183.9 6.5 %fusion.14 = (f32[512]{0:T(512)S(1)}, f32[512,1600]{0,1:T(8,128)S(1)}) fusion(bf16[1600,2048]{1,0:T(8,128)(2,1)} %get-tuple-element.320, bf16[2,512,2048]{2,1,0:T(8,128)(2,1)} %get-tuple-element.319, s32[]{:T(128)} %get-tuple-element.303), kind=kOutput, calls=%fused_computation.48.clone.1 | convolution fusion | flops 3356261888 | bytes 11930112 | tf_op jit(solution)/shard_map/while/body/eval_jaxpr/dot_general | solution.py:69
  192.0 6.4 %fusion.14 = (f32[512]{0:T(512)S(1)}, f32[512,1600]{0,1:T(8,128)S(1)}) fusion(bf16[1600,2048]{1,0:T(8,128)(2,1)} %get-tuple-element.320, bf16[2,512,2048]{2,1,0:T(8,128)(2,1)} %get-tuple-element.319, s32[]{:T(128)} %get-tuple-element.303), kind=kOutput, calls=%fused_computation.48.clone.1 | convolution fusion | flops 3356261888 | bytes 11930112 | tf_op jit(solution)/shard_map/while/body/eval_jaxpr/dot_general | solution.py:69
  200.1 40.8 %all-gather = f32[64,1,1024]{2,1,0:T(1,128)S(1)} all-gather(f32[1,1,1024]{2,1,0:T(1,128)S(1)} %reshape.60), channel_id=1, replica_groups=mesh['vocab'=64,'width'=8] {'vocab'}, dimensions={0}, use_global_device_ids=true | all-gather | bytes 266240 | tf_op jit(solution)/shard_map/all_gather | solution.py:11
  240.9 37.1 %all-gather.1 = f32[64,1,1024]{2,1,0:T(1,128)S(1)} all-gather(f32[1,1,1024]{2,1,0:T(1,128)S(1)} %reshape.62), channel_id=1, replica_groups=mesh['vocab'=64,'width'=8] {'vocab'}, dimensions={0}, use_global_device_ids=true | all-gather | bytes 266240 | tf_op jit(solution)/shard_map/all_gather | solution.py:11
  278.1 36.9 %all-gather.2 = f32[64,1,1024]{2,1,0:T(1,128)S(1)} all-gather(f32[1,1,1024]{2,1,0:T(1,128)S(1)} %reshape.64), channel_id=1, replica_groups=mesh['vocab'=64,'width'=8] {'vocab'}, dimensions={0}, use_global_device_ids=true | all-gather | bytes 266240 | tf_op jit(solution)/shard_map/all_gather | solution.py:11
  315.1 37.3 %all-gather.3 = f32[64,1,1024]{2,1,0:T(1,128)S(1)} all-gather(f32[1,1,1024]{2,1,0:T(1,128)S(1)} %reshape.66), channel_id=1, replica_groups=mesh['vocab'=64,'width'=8] {'vocab'}, dimensions={0}, use_global_device_ids=true | all-gather | bytes 266240 | tf_op jit(solution)/shard_map/all_gather | solution.py:11
  352.7 7.6 %while.33 = (s32[]{:T(128)}, f32[1024]{0:T(1024)S(1)}, f32[1024]{0:T(1024)S(1)}, f32[1024]{0:T(1024)S(1)}, f32[1024]{0:T(1024)S(1)}, /*index=5*/f32[63,1024]{1,0...) while((s32[]{:T(128)}, f32[1024]{0:T(1024)S(1)}, ...), condition=%wide.region_9.10_spmd, body=%wide.region_8.9_spmd.sunk | while | flops 16386 | bytes 110701 | solution.py:14
  360.9 96.1 %psum.15 = f32[64]{0:T(128)S(1)} all-reduce(f32[64]{0:T(128)S(1)} %select_reduce_fusion.1), channel_id=1, replica_groups=mesh['vocab'=64,'width'=8] {'vocab','width'}, use_global_device_ids=true, to_apply=%region_12.13 | all-reduce | flops 64 | bytes 512 | tf_op jit(solution)/shard_map/psum | solution.py:100
  (467 shorter events, 27.3 us)
Async XLA Ops:
  7.2 173.2 %copy-start = (bf16[1600,256]{1,0:T(8,128)(2,1)S(1)}, bf16[1600,256]{1,0:T(8,128)(2,1)}, u32[]{:S(2)}) copy-start(bf16[1600,256]{1,0:T(8,128)(2,1)} %param.12) | copy-start | bytes 2457604
  7.2 176.7 %all-gather.6.cloned.1.call-start = ((), (), s32[]{:S(2)}) async-start(), calls=%async_computation.1 | async-start | bytes 4259840 | tf_op jit(solution)/shard_map/all_gather | solution.py:51
  7.2 29.8 %collective-permute-start = (bf16[1600,256]{1,0:T(8,128)(2,1)}, bf16[1600,256]{1,0:T(8,128)(2,1)S(1)}, u32[]{:S(2)}, u32[]{:S(2)}) collective-permute-start(bf16[1600,256]{1,0:T(8,128)(2,1)} %param.12), channel_id=1, source_target_pairs={{0,1},{1,2},{2,3},{3,4},{4,5},{5,6},{6,7},{7,0},{8,9},{9,10},{10,1... | collective-permute-start | bytes 2457608 | tf_op jit(solution)/shard_map/ppermute | solution.py:61
  37.0 27.4 %collective-permute-start.1 = (bf16[1600,256]{1,0:T(8,128)(2,1)S(1)}, bf16[1600,256]{1,0:T(8,128)(2,1)S(1)}, u32[]{:S(2)}, u32[]{:S(2)}) collective-permute-start(bf16[1600,256]{1,0:T(8,128)(2,1)S(1)} %collective-permute-done), channel_id=1, source_target_pairs={{0,1},{1,2},{2,3},{3,4},{4,5},{5,6},{6,7},{7,0},{8,9},{9,10},{10,1... | collective-permute-start | bytes 2457608 | tf_op jit(solution)/shard_map/ppermute | solution.py:61
  64.4 19.6 %collective-permute-start.2 = (bf16[1600,256]{1,0:T(8,128)(2,1)S(1)}, bf16[1600,256]{1,0:T(8,128)(2,1)S(1)}, u32[]{:S(2)}, u32[]{:S(2)}) collective-permute-start(bf16[1600,256]{1,0:T(8,128)(2,1)S(1)} %collective-permute-done.1), channel_id=1, source_target_pairs={{0,1},{1,2},{2,3},{3,4},{4,5},{5,6},{6,7},{7,0},{8,9},{9,10},{10,1... | collective-permute-start | bytes 2457608 | tf_op jit(solution)/shard_map/ppermute | solution.py:61
  84.1 16.2 %collective-permute-start.3 = (bf16[1600,256]{1,0:T(8,128)(2,1)S(1)}, bf16[1600,256]{1,0:T(8,128)(2,1)S(1)}, u32[]{:S(2)}, u32[]{:S(2)}) collective-permute-start(bf16[1600,256]{1,0:T(8,128)(2,1)S(1)} %collective-permute-done.2), channel_id=1, source_target_pairs={{0,1},{1,2},{2,3},{3,4},{4,5},{5,6},{6,7},{7,0},{8,9},{9,10},{10,1... | collective-permute-start | bytes 2457608 | tf_op jit(solution)/shard_map/ppermute | solution.py:61
  100.3 0.9 copy-start.1
  101.1 15.8 %collective-permute-start.4 = (bf16[1600,256]{1,0:T(8,128)(2,1)S(1)}, bf16[1600,256]{1,0:T(8,128)(2,1)S(1)}, u32[]{:S(2)}, u32[]{:S(2)}) collective-permute-start(bf16[1600,256]{1,0:T(8,128)(2,1)S(1)} %collective-permute-done.3), channel_id=1, source_target_pairs={{0,1},{1,2},{2,3},{3,4},{4,5},{5,6},{6,7},{7,0},{8,9},{9,10},{10,1... | collective-permute-start | bytes 2457608 | tf_op jit(solution)/shard_map/ppermute | solution.py:61
  117.0 0.9 copy-start.3
  117.9 15.7 %collective-permute-start.5 = (bf16[1600,256]{1,0:T(8,128)(2,1)S(1)}, bf16[1600,256]{1,0:T(8,128)(2,1)}, u32[]{:S(2)}, u32[]{:S(2)}) collective-permute-start(bf16[1600,256]{1,0:T(8,128)(2,1)S(1)} %collective-permute-done.4), channel_id=1, source_target_pairs={{0,1},{1,2},{2,3},{3,4},{4,5},{5,6},{6,7},{7,0},{8,9},{9,10},{10,1... | collective-permute-start | bytes 2457608 | tf_op jit(solution)/shard_map/ppermute | solution.py:61
  133.6 36.9 %collective-permute-start.6 = (bf16[1600,256]{1,0:T(8,128)(2,1)}, bf16[1600,256]{1,0:T(8,128)(2,1)}, u32[]{:S(2)}, u32[]{:S(2)}) collective-permute-start(bf16[1600,256]{1,0:T(8,128)(2,1)} %collective-permute-done.5), channel_id=1, source_target_pairs={{0,1},{1,2},{2,3},{3,4},{4,5},{5,6},{6,7},{7,0},{8,9},{9,10},{10,1... | collective-permute-start | bytes 2457608 | tf_op jit(solution)/shard_map/ppermute | solution.py:61
  170.5 9.3 %copy-start.4 = (bf16[1600,256]{1,0:T(8,128)(2,1)S(1)}, bf16[1600,256]{1,0:T(8,128)(2,1)}, u32[]{:S(2)}) copy-start(bf16[1600,256]{1,0:T(8,128)(2,1)} %copy-done.3) | copy-start | bytes 2457604
  170.5 9.4 %copy-start.2 = (bf16[1600,256]{1,0:T(8,128)(2,1)S(1)}, bf16[1600,256]{1,0:T(8,128)(2,1)}, u32[]{:S(2)}) copy-start(bf16[1600,256]{1,0:T(8,128)(2,1)} %copy-done.1) | copy-start | bytes 2457604
  183.9 176.4 %copy-start.7 = (s32[16]{0:T(128)S(1)}, s32[16]{0:T(128)}, u32[]{:S(2)}) copy-start(s32[16]{0:T(128)} %param.14) | copy-start | bytes 196
  183.9 273.2 %copy-start.6 = (s32[64]{0:T(128)S(1)}, s32[64]{0:T(128)}, u32[]{:S(2)}) copy-start(s32[64]{0:T(128)} %param.15) | copy-start | bytes 772
  360.9 96.7 %copy-start.5 = (f32[16]{0:T(128)}, f32[16]{0:T(128)S(1)}, u32[]{:S(2)}) copy-start(f32[16]{0:T(128)S(1)} %get-tuple-element.158) | copy-start | bytes 196
Sparse Core Ops, SparseCore 0:
  84.2 90.0 all-gather.5
